TPU v7x, 32 devices: a whole 2x2x4 slice. The times are simulated.
32 devices in a mesh: grp: 4 (over y, x), col: 8 (over z, core).
Axes of the slice: x: 2, y: 2, z: 4, core: 2. Of those that a mesh axis runs over, the one named last changes fastest.
Arguments:
- start_block: float32 [16, 8192], P(None, ('grp', 'col')), may hold values from -6 to 6
- tile_values: float32 [4, 8, 32, 256, 256], P('grp', 'col'), may hold values from 0 to 1, as said below
- tile_row: int32 [4, 8, 32], P('grp', 'col'), may hold values from 0 to 31, as said below
- tile_col: int32 [4, 8, 32], P('grp', 'col'), may hold values from 0 to 31, as said below
- tile_count: int32 [4, 8], P('grp', 'col'), may hold values from 8 to 32, as said below
Outputs:
- basis: float32 [5, 16, 8192], P(None, None, ('grp', 'col'))
- projections: float32 [4, 4, 16, 16], replicated
- factors: float32 [5, 16, 16], replicated
Inputs may be any that keep to these rules, and one draw needn't show every extreme that they name: `tile_row`: A tile of the device at grp index g lies in tile rows g * 8 * 1 to (g + 1) * 8 - 1. `tile_col`: A tile column t of the device at col index c has (t) % 8 == c. Coordinate pairs may repeat; repeated tiles add. The live tiles of a device are its first tile_count slots; some device has all 32 slots live. `tile_values`: entries are nonnegative.
All inputs are finite; a program needn't handle non-finite values.
Results may differ from a plain program's by a relative error of at most 0.0003.
Values sent between devices are 32-bit elements; how exact they have to be, the bound alone decides.
A program may use at most 64 MiB of HBM per device.

v0:
```python
import jax
import jax.numpy as jnp
from jax import lax
from jax.sharding import PartitionSpec as P

ITERS = 4
highest = lax.Precision.HIGHEST


def select_rows(selector, panel, tile_size):
    block_rows = panel.shape[0]
    shaped = panel.reshape(block_rows, -1, tile_size)
    return jnp.einsum("sr,qrt->qst", selector, shaped, precision=highest)


def spread_rows(selector, pieces):
    block_rows = pieces.shape[0]
    placed = jnp.einsum("sr,qst->qrt", selector, pieces, precision=highest)
    return placed.reshape(block_rows, -1)


def orthonormal(block_rows, gram_now):
    factor = jnp.linalg.cholesky(gram_now)
    solved = jax.scipy.linalg.solve_triangular(factor, block_rows, lower=True)
    return (solved, factor)


def body(start_block, tile_values, tile_row, tile_col, tile_count):
    grp_size = lax.axis_size("grp")
    col_size = lax.axis_size("col")
    grp_index = lax.axis_index("grp")
    tile_data = tile_values[0, 0]
    tile_size = tile_data.shape[-1]
    slot_count = tile_data.shape[0]
    shard_len = start_block.shape[1]
    row_tiles = shard_len // tile_size
    node_total = shard_len * grp_size * col_size
    live_slot = (jnp.arange(slot_count, dtype=jnp.int32) < tile_count[0, 0]).astype(jnp.float32)
    local_row = tile_row[0, 0] - grp_index * (col_size * row_tiles)
    global_col = tile_col[0, 0]
    local_col = global_col // (row_tiles * col_size) * row_tiles + global_col % row_tiles
    row_places = jnp.arange(col_size * row_tiles, dtype=jnp.int32)
    col_places = jnp.arange(grp_size * row_tiles, dtype=jnp.int32)
    row_select = (local_row[:, None] == row_places[None, :]).astype(jnp.float32) * live_slot[
        :, None
    ]
    col_select = (local_col[:, None] == col_places[None, :]).astype(jnp.float32) * live_slot[
        :, None
    ]

    def combine(part_rows, part_cols):
        mine_rows = lax.psum_scatter(part_rows, "col", scatter_dimension=1, tiled=True)
        mine_cols = lax.psum_scatter(part_cols, "grp", scatter_dimension=1, tiled=True)
        return mine_rows + mine_cols

    row_totals = jnp.sum(tile_data, axis=2)[None]
    col_totals = jnp.sum(tile_data, axis=1)[None]
    degree = combine(spread_rows(row_select, row_totals), spread_rows(col_select, col_totals))
    start_gram = (
        lax.psum(jnp.dot(start_block, start_block.T, precision=highest), ("grp", "col"))
        / node_total
    )
    first_block, factor = orthonormal(start_block, start_gram)
    block_width = start_block.shape[0]
    basis_list = [first_block]
    factor_list = [factor]
    projections = jnp.zeros((ITERS, ITERS, block_width, block_width), jnp.float32)
    for step_index in range(ITERS):
        laplace_vector = basis_list[-1]
        row_panel = lax.all_gather(laplace_vector, "col", axis=1, tiled=True)
        col_panel = lax.all_gather(laplace_vector, "grp", axis=1, tiled=True)
        at_cols = select_rows(col_select, col_panel, tile_size)
        at_rows = select_rows(row_select, row_panel, tile_size)
        into_rows = jnp.einsum("sij,qsj->qsi", tile_data, at_cols, precision=highest)
        into_cols = jnp.einsum("sij,qsi->qsj", tile_data, at_rows, precision=highest)
        product = combine(spread_rows(row_select, into_rows), spread_rows(col_select, into_cols))
        applied = degree * laplace_vector - product
        stacked = jnp.stack(basis_list)
        coeff_part = jnp.einsum("an,jbn->jab", applied, stacked, precision=highest)
        coeffs = lax.psum(coeff_part, ("grp", "col")) / node_total
        applied = applied - jnp.einsum("jab,jbn->an", coeffs, stacked, precision=highest)
        gram_now = (
            lax.psum(jnp.dot(applied, applied.T, precision=highest), ("grp", "col")) / node_total
        )
        next_block, factor = orthonormal(applied, gram_now)
        basis_list.append(next_block)
        factor_list.append(factor)
        projections = projections.at[step_index, : step_index + 1].set(coeffs)
    return (jnp.stack(basis_list), projections, jnp.stack(factor_list))


def solution(mesh):
    in_specs = (
        P(None, ("grp", "col")),
        P("grp", "col", None, None, None),
        P("grp", "col", None),
        P("grp", "col", None),
        P("grp", "col"),
    )
    out_specs = (P(None, None, ("grp", "col")), P(), P())
    return jax.shard_map(body, mesh=mesh, in_specs=in_specs, out_specs=out_specs, check_vma=False)
```

profile of v0, /device:TPU:0, one launch (start us, length us, event | category | flops | bytes accessed | tf_op | source)
XLA Modules:
  0.0 785.5 jit_solution(12459310264060773894)
XLA Ops:
  8.6 4.6 fusion.180
  13.5 0.9 bitcast_bitcast_fusion.1
  15.0 1.1 bitcast_bitcast_fusion
  16.3 42.0 %psum.63 = f32[16,16]{0,1:T(8,128)S(1)} all-reduce(f32[16,16]{0,1:T(8,128)S(1)} %fusion.181), channel_id=1, replica_groups=mesh['grp'=4,'col'=8] {'grp','col'}, use_global_device_ids=true, to_apply=%region_0.1 | all-reduce | flops 256 | bytes 2048 | tf_op jit(solution)/shard_map/psum | solution.py:60
  58.3 1.5 cholesky.89
  61.1 1.2 custom-call.9
  62.6 14.2 %all_gather.25 = f32[16,2048]{1,0:T(8,128)S(1)} all-gather(f32[16,256]{1,0:T(8,128)S(1)} %get-tuple-element.65), channel_id=1, replica_groups=mesh['grp'=4,'col'=8] {'col'}, dimensions={1}, use_global_device_ids=true | all-gather | bytes 147456 | tf_op jit(solution)/shard_map/all_gather | solution.py:70
  77.4 6.7 fusion.19
  84.1 0.7 fusion.62
  85.5 9.1 %all_gather.24 = f32[16,1024]{1,0:T(8,128)S(1)} all-gather(f32[16,256]{1,0:T(8,128)S(1)} %get-tuple-element.65), channel_id=1, replica_groups=mesh['grp'=4,'col'=8] {'grp'}, dimensions={1}, use_global_device_ids=true | all-gather | bytes 81920 | tf_op jit(solution)/shard_map/all_gather | solution.py:71
  95.3 9.5 %fusion.16 = f32[16,32,256]{2,0,1:T(8,128)S(1)} fusion(f32[1,1,32,256,256]{4,3,2,1,0:T(8,128)} %param.17, f32[16,32,256]{2,1,0:T(8,128)S(1)} %convolution_bitcast_fusion.7), kind=kOutput, calls=%fused_computation.16 | convolution fusion | flops 402653184 | bytes 9437184 | tf_op jit(solution)/shard_map/sij,qsj->qsi/dot_general | solution.py:74
  104.8 0.7 fusion.65
  105.5 0.7 copy.82
  107.4 1.0 copy.77
  108.4 1.0 copy.75
  109.4 33.3 %reduce-scatter.15.cloned.1.call-done = f32[16,256]{1,0:T(8,128)} async-done(((f32[16,2048]{1,0:T(8,128)}), f32[16,256]{1,0:T(8,128)}) %reduce-scatter.15.cloned.1.call-update) | async-done | bytes 16400 | tf_op jit(solution)/shard_map/reduce_scatter | solution.py:52
  142.6 0.9 convolution_bitcast_fusion.15
  143.5 37.9 %psum.64 = f32[1,16,16]{1,2,0:T(8,128)S(1)} all-reduce(f32[1,16,16]{1,2,0:T(8,128)S(1)} %convolution_bitcast_fusion.15), channel_id=1, replica_groups=mesh['grp'=4,'col'=8] {'grp','col'}, use_global_device_ids=true, to_apply=%region_9.12 | all-reduce | flops 256 | bytes 2048 | tf_op jit(solution)/shard_map/psum | solution.py:80
  181.4 0.9 convolution_subtract_fusion
  182.5 41.3 %psum.65 = f32[16,16]{0,1:T(8,128)S(1)} all-reduce(f32[16,16]{0,1:T(8,128)S(1)} %fusion.182), channel_id=1, replica_groups=mesh['grp'=4,'col'=8] {'grp','col'}, use_global_device_ids=true, to_apply=%region_10.13 | all-reduce | flops 256 | bytes 2048 | tf_op jit(solution)/shard_map/psum | solution.py:83
  223.8 1.5 cholesky.100
  226.6 1.2 custom-call.10
  228.1 9.0 %all_gather.26 = f32[16,1024]{1,0:T(8,128)S(1)} all-gather(f32[16,256]{1,0:T(8,128)S(1)} %get-tuple-element.67), channel_id=1, replica_groups=mesh['grp'=4,'col'=8] {'grp'}, dimensions={1}, use_global_device_ids=true | all-gather | bytes 81920 | tf_op jit(solution)/shard_map/all_gather | solution.py:71
  237.1 13.9 %all_gather.27 = f32[16,2048]{1,0:T(8,128)S(1)} all-gather(f32[16,256]{1,0:T(8,128)S(1)} %get-tuple-element.67), channel_id=1, replica_groups=mesh['grp'=4,'col'=8] {'col'}, dimensions={1}, use_global_device_ids=true | all-gather | bytes 147456 | tf_op jit(solution)/shard_map/all_gather | solution.py:70
  251.7 9.5 %fusion.22 = f32[16,32,256]{2,0,1:T(8,128)S(1)} fusion(f32[1,1,32,256,256]{4,3,2,1,0:T(8,128)} %param.17, f32[16,32,256]{2,1,0:T(8,128)S(1)} %convolution_bitcast_fusion.6), kind=kOutput, calls=%fused_computation.18 | convolution fusion | flops 402653184 | bytes 9437184 | tf_op jit(solution)/shard_map/sij,qsj->qsi/dot_general | solution.py:74
  261.8 6.6 fusion.25
  268.5 0.7 fusion.56
  269.9 0.7 fusion.59
  270.6 0.7 copy.85
  272.0 20.4 %reduce-scatter.21.cloned.1.call-done = f32[16,256]{1,0:T(8,128)} async-done(((f32[16,1024]{1,0:T(8,128)}), f32[16,256]{1,0:T(8,128)}) %reduce-scatter.21.cloned.1.call-update) | async-done | bytes 16400 | tf_op jit(solution)/shard_map/reduce_scatter | solution.py:53
  292.4 33.3 %reduce-scatter.19.cloned.1.call-done = f32[16,256]{1,0:T(8,128)} async-done(((f32[16,2048]{1,0:T(8,128)}), f32[16,256]{1,0:T(8,128)}) %reduce-scatter.19.cloned.1.call-update) | async-done | bytes 16400 | tf_op jit(solution)/shard_map/reduce_scatter | solution.py:52
  325.7 0.7 add_subtract_fusion.2
  326.6 37.8 %psum.66 = f32[2,16,16]{1,2,0:T(8,128)S(1)} all-reduce(f32[2,16,16]{1,2,0:T(8,128)S(1)} %convolution_bitcast_fusion.14), channel_id=1, replica_groups=mesh['grp'=4,'col'=8] {'grp','col'}, use_global_device_ids=true, to_apply=%region_13.16 | all-reduce | flops 512 | bytes 4096 | tf_op jit(solution)/shard_map/psum | solution.py:80
  364.8 41.6 %psum.67 = f32[16,16]{0,1:T(8,128)S(1)} all-reduce(f32[16,16]{0,1:T(8,128)S(1)} %fusion.183), channel_id=1, replica_groups=mesh['grp'=4,'col'=8] {'grp','col'}, use_global_device_ids=true, to_apply=%region_14.17 | all-reduce | flops 256 | bytes 2048 | tf_op jit(solution)/shard_map/psum | solution.py:83
  406.5 1.5 cholesky.111
  409.3 1.2 custom-call.11
  410.7 9.0 %all_gather.28 = f32[16,1024]{1,0:T(8,128)S(1)} all-gather(f32[16,256]{1,0:T(8,128)S(1)} %get-tuple-element.69), channel_id=1, replica_groups=mesh['grp'=4,'col'=8] {'grp'}, dimensions={1}, use_global_device_ids=true | all-gather | bytes 81920 | tf_op jit(solution)/shard_map/all_gather | solution.py:71
  419.7 13.9 %all_gather.29 = f32[16,2048]{1,0:T(8,128)S(1)} all-gather(f32[16,256]{1,0:T(8,128)S(1)} %get-tuple-element.69), channel_id=1, replica_groups=mesh['grp'=4,'col'=8] {'col'}, dimensions={1}, use_global_device_ids=true | all-gather | bytes 147456 | tf_op jit(solution)/shard_map/all_gather | solution.py:70
  434.3 9.5 %fusion.28 = f32[16,32,256]{2,0,1:T(8,128)S(1)} fusion(f32[1,1,32,256,256]{4,3,2,1,0:T(8,128)} %param.17, f32[16,32,256]{2,1,0:T(8,128)S(1)} %convolution_bitcast_fusion.5), kind=kOutput, calls=%fused_computation.20 | convolution fusion | flops 402653184 | bytes 9437184 | tf_op jit(solution)/shard_map/sij,qsj->qsi/dot_general | solution.py:74
  444.5 6.6 fusion.31
  451.1 0.7 fusion.50
  452.5 0.7 fusion.53
  453.2 0.7 copy.88
  454.7 20.3 %reduce-scatter.25.cloned.1.call-done = f32[16,256]{1,0:T(8,128)} async-done(((f32[16,1024]{1,0:T(8,128)}), f32[16,256]{1,0:T(8,128)}) %reduce-scatter.25.cloned.1.call-update) | async-done | bytes 16400 | tf_op jit(solution)/shard_map/reduce_scatter | solution.py:53
  474.9 33.5 %reduce-scatter.23.cloned.1.call-done = f32[16,256]{1,0:T(8,128)} async-done(((f32[16,2048]{1,0:T(8,128)}), f32[16,256]{1,0:T(8,128)}) %reduce-scatter.23.cloned.1.call-update) | async-done | bytes 16400 | tf_op jit(solution)/shard_map/reduce_scatter | solution.py:52
  508.4 0.7 add_subtract_fusion.1
  509.4 37.9 %psum.68 = f32[3,16,16]{1,2,0:T(8,128)S(1)} all-reduce(f32[3,16,16]{1,2,0:T(8,128)S(1)} %convolution_bitcast_fusion.9), channel_id=1, replica_groups=mesh['grp'=4,'col'=8] {'grp','col'}, use_global_device_ids=true, to_apply=%region_17.20 | all-reduce | flops 768 | bytes 6144 | tf_op jit(solution)/shard_map/psum | solution.py:80
  547.6 41.4 %psum.69 = f32[16,16]{0,1:T(8,128)S(1)} all-reduce(f32[16,16]{0,1:T(8,128)S(1)} %fusion.184), channel_id=1, replica_groups=mesh['grp'=4,'col'=8] {'grp','col'}, use_global_device_ids=true, to_apply=%region_18.21 | all-reduce | flops 256 | bytes 2048 | tf_op jit(solution)/shard_map/psum | solution.py:83
  589.1 1.5 cholesky.122
  591.9 1.2 custom-call.12
  593.3 9.0 %all_gather.30 = f32[16,1024]{1,0:T(8,128)S(1)} all-gather(f32[16,256]{1,0:T(8,128)S(1)} %get-tuple-element.71), channel_id=1, replica_groups=mesh['grp'=4,'col'=8] {'grp'}, dimensions={1}, use_global_device_ids=true | all-gather | bytes 81920 | tf_op jit(solution)/shard_map/all_gather | solution.py:71
  602.4 14.2 %all_gather.31 = f32[16,2048]{1,0:T(8,128)S(1)} all-gather(f32[16,256]{1,0:T(8,128)S(1)} %get-tuple-element.71), channel_id=1, replica_groups=mesh['grp'=4,'col'=8] {'col'}, dimensions={1}, use_global_device_ids=true | all-gather | bytes 147456 | tf_op jit(solution)/shard_map/all_gather | solution.py:70
  617.2 9.5 %fusion.34 = f32[16,32,256]{2,0,1:T(8,128)S(1)} fusion(f32[1,1,32,256,256]{4,3,2,1,0:T(8,128)} %param.17, f32[16,32,256]{2,1,0:T(8,128)S(1)} %convolution_bitcast_fusion.4), kind=kOutput, calls=%fused_computation.22 | convolution fusion | flops 402653184 | bytes 9437184 | tf_op jit(solution)/shard_map/sij,qsj->qsi/dot_general | solution.py:74
  627.3 6.6 fusion.37
  635.4 0.7 fusion.47
  636.1 0.7 copy.91
  637.5 20.4 %reduce-scatter.29.cloned.1.call-done = f32[16,256]{1,0:T(8,128)} async-done(((f32[16,1024]{1,0:T(8,128)}), f32[16,256]{1,0:T(8,128)}) %reduce-scatter.29.cloned.1.call-update) | async-done | bytes 16400 | tf_op jit(solution)/shard_map/reduce_scatter | solution.py:53
  657.8 33.3 %reduce-scatter.27.cloned.1.call-done = f32[16,256]{1,0:T(8,128)} async-done(((f32[16,2048]{1,0:T(8,128)}), f32[16,256]{1,0:T(8,128)}) %reduce-scatter.27.cloned.1.call-update) | async-done | bytes 16400 | tf_op jit(solution)/shard_map/reduce_scatter | solution.py:52
  691.1 0.7 add_subtract_fusion
  692.0 37.9 %psum.70 = f32[4,16,16]{1,2,0:T(8,128)S(1)} all-reduce(f32[4,16,16]{1,2,0:T(8,128)S(1)} %convolution_bitcast_fusion.8), channel_id=1, replica_groups=mesh['grp'=4,'col'=8] {'grp','col'}, use_global_device_ids=true, to_apply=%region_21.24 | all-reduce | flops 1024 | bytes 8192 | tf_op jit(solution)/shard_map/psum | solution.py:80
  730.3 41.4 %psum.71 = f32[16,16]{0,1:T(8,128)S(1)} all-reduce(f32[16,16]{0,1:T(8,128)S(1)} %fusion.185), channel_id=1, replica_groups=mesh['grp'=4,'col'=8] {'grp','col'}, use_global_device_ids=true, to_apply=%region_22.25 | all-reduce | flops 256 | bytes 2048 | tf_op jit(solution)/shard_map/psum | solution.py:83
  771.8 1.5 cholesky.133
  774.6 1.2 custom-call.13
  775.8 0.8 copy.65
  (118 shorter events, 25.3 us)
Async XLA Ops:
  7.2 9.0 %copy-start = (f32[16,256]{1,0:T(8,128)S(1)}, f32[16,256]{1,0:T(8,128)}, u32[]{:S(2)}) copy-start(f32[16,256]{1,0:T(8,128)} %param.16) | copy-start | bytes 49156
  7.2 7.3 copy-start.3
  7.2 100.2 %reduce-scatter.33.cloned.1.call-start = ((), (), s32[]{:S(2)}) async-start(), calls=%async_computation.19 | async-start | bytes 655360
  14.4 94.0 %reduce-scatter.31.cloned.1.call-start = ((), (), s32[]{:S(2)}) async-start(), calls=%async_computation.18 | async-start | bytes 1179648
  16.1 93.3 %reduce-scatter.17.cloned.1.call-start = ((), (), s32[]{:S(2)}) async-start(), calls=%async_computation.11 | async-start | bytes 81920 | tf_op jit(solution)/shard_map/reduce_scatter | solution.py:53
  85.4 57.2 %reduce-scatter.15.cloned.1.call-start = ((), (), s32[]{:S(2)}) async-start(), calls=%async_computation.10 | async-start | bytes 147456 | tf_op jit(solution)/shard_map/reduce_scatter | solution.py:52
  106.2 186.2 %reduce-scatter.21.cloned.1.call-start = ((), (), s32[]{:S(2)}) async-start(), calls=%async_computation.13 | async-start | bytes 81920 | tf_op jit(solution)/shard_map/reduce_scatter | solution.py:53
  269.9 55.9 %reduce-scatter.19.cloned.1.call-start = ((), (), s32[]{:S(2)}) async-start(), calls=%async_computation.12 | async-start | bytes 147456 | tf_op jit(solution)/shard_map/reduce_scatter | solution.py:52
  271.3 203.6 %reduce-scatter.25.cloned.1.call-start = ((), (), s32[]{:S(2)}) async-start(), calls=%async_computation.15 | async-start | bytes 81920 | tf_op jit(solution)/shard_map/reduce_scatter | solution.py:53
  452.5 55.9 %reduce-scatter.23.cloned.1.call-start = ((), (), s32[]{:S(2)}) async-start(), calls=%async_computation.14 | async-start | bytes 147456 | tf_op jit(solution)/shard_map/reduce_scatter | solution.py:52
  453.9 203.9 %reduce-scatter.29.cloned.1.call-start = ((), (), s32[]{:S(2)}) async-start(), calls=%async_computation.17 | async-start | bytes 81920 | tf_op jit(solution)/shard_map/reduce_scatter | solution.py:53
  635.3 55.8 %reduce-scatter.27.cloned.1.call-start = ((), (), s32[]{:S(2)}) async-start(), calls=%async_computation.16 | async-start | bytes 147456 | tf_op jit(solution)/shard_map/reduce_scatter | solution.py:52
  777.2 0.6 copy-start.2
  777.8 0.6 copy-start.1
Sparse Core Ops, SparseCore 0:
  14.5 27.8 reduce-scatter.32
  44.6 32.9 reduce-scatter.30
  85.6 23.7 reduce-scatter.16
  112.0 30.5 reduce-scatter.14
  270.0 22.3 reduce-scatter.20
  295.1 30.5 reduce-scatter.18
  452.6 22.2 reduce-scatter.24
  477.7 30.6 reduce-scatter.22
  635.5 22.3 reduce-scatter.28
  660.5 30.5 reduce-scatter.26
where the time goes:
time: 797 us; the launch traced here: 786 us
  blocking collectives  452 us (57%)
  waiting for transfers between devices  195 us (24%)
  matrix products  79.7 us (10%)
  other arithmetic  30.8 us (4%)
  between operations  15.5 us (2%)
  local copies, waits for them, and re-layouts  12.4 us (2%)
    psum x4, blocking collectives, body(): lax.psum(jnp.dot(applied, applied.T, precision=highest), ('grp', 'col'))  166 us
    psum x4, blocking collectives, body(): coeffs = lax.psum(coeff_part, ('grp', 'col')) / node_total  152 us
    reduce_scatter x4, waiting for transfers between devices, combine(): lax.psum_scatter(part_rows, 'col', scatter_dimension=1, tiled=True)  133 us
    reduce_scatter x4, waiting for transfers between devices, combine(): lax.psum_scatter(part_cols, 'grp', scatter_dimension=1, tiled=True)  61 us
    all_gather x4, blocking collectives, body(): row_panel = lax.all_gather(laplace_vector, 'col', axis=1, tiled=True)  56.3 us
    psum x1, blocking collectives, body(): lax.psum(jnp.dot(start_block, start_block.T, precision=highest), ('grp',...  42 us
    dot_general x4, matrix products, body(): jnp.einsum('sij,qsj->qsi', tile_data, at_cols, precision=highest)  37.9 us
    all_gather x4, blocking collectives, body(): col_panel = lax.all_gather(laplace_vector, 'grp', axis=1, tiled=True)  36.2 us
  transfers between devices with their start and end apart: 10, of which 7 were waited for; matrix products, arithmetic and copies ran while one was open for 4% of the time, Pallas kernels for 0%

commit v1 on v0

--- a/solution.py
+++ b/solution.py
@@ -57,7 +57,7 @@
     col_totals = jnp.sum(tile_data, axis=1)[None]
     degree = combine(spread_rows(row_select, row_totals), spread_rows(col_select, col_totals))
     start_gram = (
-        lax.psum(jnp.dot(start_block, start_block.T, precision=highest), ("grp", "col"))
+        lax.psum(lax.psum(jnp.dot(start_block, start_block.T, precision=highest), "grp"), "col")
         / node_total
     )
     first_block, factor = orthonormal(start_block, start_gram)

time: 797 us -> 790 us (level)
  blocking collectives: 452 us -> 435 us
  waiting for transfers between devices: 195 us -> 206 us
    psum x1 -> x2, blocking collectives: 42 us -> 26.5 us  [the longest x1 14.9 us: body(): lax.psum(lax.psum(jnp.dot(start_block, start_block.T, precision=highest),...]
    reduce_scatter x4, waiting for transfers between devices: 61 us -> 72.6 us  [combine(): lax.psum_scatter(part_cols, 'grp', scatter_dimension=1, tiled=True)]
  transfers between devices with their start and end apart: 10 -> 10, of which waited for: 7 -> 8; matrix products, arithmetic and copies ran while one was open for 4% -> 4% of each run, Pallas kernels for 0% -> 0%
where the time goes in v1:
time: 790 us; the launch traced here: 780 us
  blocking collectives  435 us (55%)
  waiting for transfers between devices  206 us (26%)
  matrix products  79.8 us (10%)
  other arithmetic  30.8 us (4%)
  between operations  15.6 us (2%)
  local copies, waits for them, and re-layouts  12.4 us (2%)
    psum x4, blocking collectives, body(): lax.psum(jnp.dot(applied, applied.T, precision=highest), ('grp', 'col'))  166 us
    psum x4, blocking collectives, body(): coeffs = lax.psum(coeff_part, ('grp', 'col')) / node_total  152 us
    reduce_scatter x4, waiting for transfers between devices, combine(): lax.psum_scatter(part_rows, 'col', scatter_dimension=1, tiled=True)  133 us
    reduce_scatter x4, waiting for transfers between devices, combine(): lax.psum_scatter(part_cols, 'grp', scatter_dimension=1, tiled=True)  72.6 us
    all_gather x4, blocking collectives, body(): row_panel = lax.all_gather(laplace_vector, 'col', axis=1, tiled=True)  56.2 us
    dot_general x4, matrix products, body(): jnp.einsum('sij,qsj->qsi', tile_data, at_cols, precision=highest)  37.9 us
    all_gather x4, blocking collectives, body(): col_panel = lax.all_gather(laplace_vector, 'grp', axis=1, tiled=True)  34.3 us
    dot_general x4, matrix products, body(): jnp.einsum('sij,qsi->qsj', tile_data, at_rows, precision=highest)  26.6 us
  transfers between devices with their start and end apart: 10, of which 8 were waited for; matrix products, arithmetic and copies ran while one was open for 4% of the time, Pallas kernels for 0%

profile of v1, /device:TPU:0, one launch (start us, length us, event | category | flops | bytes accessed | tf_op | source)
XLA Modules:
  0.0 779.7 jit_solution(1161211626038431396)
XLA Ops:
  8.6 4.6 fusion.180
  13.5 0.9 bitcast_bitcast_fusion.1
  15.0 1.1 bitcast_bitcast_fusion
  16.3 11.6 %psum.70 = f32[16,16]{0,1:T(8,128)S(1)} all-reduce(f32[16,16]{0,1:T(8,128)S(1)} %fusion.181), channel_id=1, replica_groups=mesh['grp'=4,'col'=8] {'grp'}, use_global_device_ids=true, to_apply=%region_0.1 | all-reduce | flops 256 | bytes 2048 | tf_op jit(solution)/shard_map/psum | solution.py:60
  27.9 14.9 %psum.71 = f32[16,16]{0,1:T(8,128)S(1)} all-reduce(f32[16,16]{0,1:T(8,128)S(1)} %psum.70), channel_id=1, replica_groups=mesh['grp'=4,'col'=8] {'col'}, use_global_device_ids=true, to_apply=%region_1.2 | all-reduce | flops 256 | bytes 2048 | tf_op jit(solution)/shard_map/psum | solution.py:60
  42.9 1.5 cholesky.89
  45.7 1.2 custom-call.9
  47.1 14.1 %all_gather.25 = f32[16,2048]{1,0:T(8,128)S(1)} all-gather(f32[16,256]{1,0:T(8,128)S(1)} %get-tuple-element.65), channel_id=1, replica_groups=mesh['grp'=4,'col'=8] {'col'}, dimensions={1}, use_global_device_ids=true | all-gather | bytes 147456 | tf_op jit(solution)/shard_map/all_gather | solution.py:70
  61.9 6.7 fusion.19
  68.6 0.7 fusion.62
  70.0 7.2 all_gather.24
  77.8 9.5 %fusion.16 = f32[16,32,256]{2,0,1:T(8,128)S(1)} fusion(f32[1,1,32,256,256]{4,3,2,1,0:T(8,128)} %param.17, f32[16,32,256]{2,1,0:T(8,128)S(1)} %convolution_bitcast_fusion.7), kind=kOutput, calls=%fused_computation.16 | convolution fusion | flops 402653184 | bytes 9437184 | tf_op jit(solution)/shard_map/sij,qsj->qsi/dot_general | solution.py:74
  87.3 0.7 fusion.65
  88.0 0.7 copy.82
  89.5 1.0 copy.77
  90.5 1.0 copy.75
  91.5 11.6 %reduce-scatter.17.cloned.1.call-done = f32[16,256]{1,0:T(8,128)} async-done(((f32[16,1024]{1,0:T(8,128)}), f32[16,256]{1,0:T(8,128)}) %reduce-scatter.17.cloned.1.call-update) | async-done | bytes 16400 | tf_op jit(solution)/shard_map/reduce_scatter | solution.py:53
  103.1 33.3 %reduce-scatter.15.cloned.1.call-done = f32[16,256]{1,0:T(8,128)} async-done(((f32[16,2048]{1,0:T(8,128)}), f32[16,256]{1,0:T(8,128)}) %reduce-scatter.15.cloned.1.call-update) | async-done | bytes 16400 | tf_op jit(solution)/shard_map/reduce_scatter | solution.py:52
  136.3 0.9 convolution_bitcast_fusion.15
  137.2 38.3 %psum.72 = f32[1,16,16]{1,2,0:T(8,128)S(1)} all-reduce(f32[1,16,16]{1,2,0:T(8,128)S(1)} %convolution_bitcast_fusion.15), channel_id=1, replica_groups=mesh['grp'=4,'col'=8] {'grp','col'}, use_global_device_ids=true, to_apply=%region_10.13 | all-reduce | flops 256 | bytes 2048 | tf_op jit(solution)/shard_map/psum | solution.py:80
  175.5 0.9 convolution_subtract_fusion
  176.6 41.4 %psum.73 = f32[16,16]{0,1:T(8,128)S(1)} all-reduce(f32[16,16]{0,1:T(8,128)S(1)} %fusion.182), channel_id=1, replica_groups=mesh['grp'=4,'col'=8] {'grp','col'}, use_global_device_ids=true, to_apply=%region_11.14 | all-reduce | flops 256 | bytes 2048 | tf_op jit(solution)/shard_map/psum | solution.py:83
  218.1 1.5 cholesky.100
  220.8 1.2 custom-call.10
  222.3 9.0 %all_gather.26 = f32[16,1024]{1,0:T(8,128)S(1)} all-gather(f32[16,256]{1,0:T(8,128)S(1)} %get-tuple-element.67), channel_id=1, replica_groups=mesh['grp'=4,'col'=8] {'grp'}, dimensions={1}, use_global_device_ids=true | all-gather | bytes 81920 | tf_op jit(solution)/shard_map/all_gather | solution.py:71
  231.3 13.9 %all_gather.27 = f32[16,2048]{1,0:T(8,128)S(1)} all-gather(f32[16,256]{1,0:T(8,128)S(1)} %get-tuple-element.67), channel_id=1, replica_groups=mesh['grp'=4,'col'=8] {'col'}, dimensions={1}, use_global_device_ids=true | all-gather | bytes 147456 | tf_op jit(solution)/shard_map/all_gather | solution.py:70
  245.9 9.5 %fusion.22 = f32[16,32,256]{2,0,1:T(8,128)S(1)} fusion(f32[1,1,32,256,256]{4,3,2,1,0:T(8,128)} %param.17, f32[16,32,256]{2,1,0:T(8,128)S(1)} %convolution_bitcast_fusion.6), kind=kOutput, calls=%fused_computation.18 | convolution fusion | flops 402653184 | bytes 9437184 | tf_op jit(solution)/shard_map/sij,qsj->qsi/dot_general | solution.py:74
  256.1 6.6 fusion.25
  262.7 0.7 fusion.56
  264.1 0.7 fusion.59
  264.8 0.7 copy.85
  266.3 20.3 %reduce-scatter.21.cloned.1.call-done = f32[16,256]{1,0:T(8,128)} async-done(((f32[16,1024]{1,0:T(8,128)}), f32[16,256]{1,0:T(8,128)}) %reduce-scatter.21.cloned.1.call-update) | async-done | bytes 16400 | tf_op jit(solution)/shard_map/reduce_scatter | solution.py:53
  286.6 33.3 %reduce-scatter.19.cloned.1.call-done = f32[16,256]{1,0:T(8,128)} async-done(((f32[16,2048]{1,0:T(8,128)}), f32[16,256]{1,0:T(8,128)}) %reduce-scatter.19.cloned.1.call-update) | async-done | bytes 16400 | tf_op jit(solution)/shard_map/reduce_scatter | solution.py:52
  319.9 0.7 add_subtract_fusion.2
  320.8 37.8 %psum.74 = f32[2,16,16]{1,2,0:T(8,128)S(1)} all-reduce(f32[2,16,16]{1,2,0:T(8,128)S(1)} %convolution_bitcast_fusion.14), channel_id=1, replica_groups=mesh['grp'=4,'col'=8] {'grp','col'}, use_global_device_ids=true, to_apply=%region_14.17 | all-reduce | flops 512 | bytes 4096 | tf_op jit(solution)/shard_map/psum | solution.py:80
  358.9 41.6 %psum.75 = f32[16,16]{0,1:T(8,128)S(1)} all-reduce(f32[16,16]{0,1:T(8,128)S(1)} %fusion.183), channel_id=1, replica_groups=mesh['grp'=4,'col'=8] {'grp','col'}, use_global_device_ids=true, to_apply=%region_15.18 | all-reduce | flops 256 | bytes 2048 | tf_op jit(solution)/shard_map/psum | solution.py:83
  400.6 1.5 cholesky.111
  403.4 1.2 custom-call.11
  404.8 9.0 %all_gather.28 = f32[16,1024]{1,0:T(8,128)S(1)} all-gather(f32[16,256]{1,0:T(8,128)S(1)} %get-tuple-element.69), channel_id=1, replica_groups=mesh['grp'=4,'col'=8] {'grp'}, dimensions={1}, use_global_device_ids=true | all-gather | bytes 81920 | tf_op jit(solution)/shard_map/all_gather | solution.py:71
  413.8 13.9 %all_gather.29 = f32[16,2048]{1,0:T(8,128)S(1)} all-gather(f32[16,256]{1,0:T(8,128)S(1)} %get-tuple-element.69), channel_id=1, replica_groups=mesh['grp'=4,'col'=8] {'col'}, dimensions={1}, use_global_device_ids=true | all-gather | bytes 147456 | tf_op jit(solution)/shard_map/all_gather | solution.py:70
  428.5 9.5 %fusion.28 = f32[16,32,256]{2,0,1:T(8,128)S(1)} fusion(f32[1,1,32,256,256]{4,3,2,1,0:T(8,128)} %param.17, f32[16,32,256]{2,1,0:T(8,128)S(1)} %convolution_bitcast_fusion.5), kind=kOutput, calls=%fused_computation.20 | convolution fusion | flops 402653184 | bytes 9437184 | tf_op jit(solution)/shard_map/sij,qsj->qsi/dot_general | solution.py:74
  438.6 6.6 fusion.31
  445.3 0.7 fusion.50
  447.4 0.7 copy.88
  448.8 20.3 %reduce-scatter.25.cloned.1.call-done = f32[16,256]{1,0:T(8,128)} async-done(((f32[16,1024]{1,0:T(8,128)}), f32[16,256]{1,0:T(8,128)}) %reduce-scatter.25.cloned.1.call-update) | async-done | bytes 16400 | tf_op jit(solution)/shard_map/reduce_scatter | solution.py:53
  469.1 33.4 %reduce-scatter.23.cloned.1.call-done = f32[16,256]{1,0:T(8,128)} async-done(((f32[16,2048]{1,0:T(8,128)}), f32[16,256]{1,0:T(8,128)}) %reduce-scatter.23.cloned.1.call-update) | async-done | bytes 16400 | tf_op jit(solution)/shard_map/reduce_scatter | solution.py:52
  502.5 0.7 add_subtract_fusion.1
  503.4 38.0 %psum.76 = f32[3,16,16]{1,2,0:T(8,128)S(1)} all-reduce(f32[3,16,16]{1,2,0:T(8,128)S(1)} %convolution_bitcast_fusion.9), channel_id=1, replica_groups=mesh['grp'=4,'col'=8] {'grp','col'}, use_global_device_ids=true, to_apply=%region_18.21 | all-reduce | flops 768 | bytes 6144 | tf_op jit(solution)/shard_map/psum | solution.py:80
  541.8 41.4 %psum.77 = f32[16,16]{0,1:T(8,128)S(1)} all-reduce(f32[16,16]{0,1:T(8,128)S(1)} %fusion.184), channel_id=1, replica_groups=mesh['grp'=4,'col'=8] {'grp','col'}, use_global_device_ids=true, to_apply=%region_19.22 | all-reduce | flops 256 | bytes 2048 | tf_op jit(solution)/shard_map/psum | solution.py:83
  583.2 1.5 cholesky.122
  586.0 1.2 custom-call.12
  587.5 9.0 %all_gather.30 = f32[16,1024]{1,0:T(8,128)S(1)} all-gather(f32[16,256]{1,0:T(8,128)S(1)} %get-tuple-element.71), channel_id=1, replica_groups=mesh['grp'=4,'col'=8] {'grp'}, dimensions={1}, use_global_device_ids=true | all-gather | bytes 81920 | tf_op jit(solution)/shard_map/all_gather | solution.py:71
  596.5 14.2 %all_gather.31 = f32[16,2048]{1,0:T(8,128)S(1)} all-gather(f32[16,256]{1,0:T(8,128)S(1)} %get-tuple-element.71), channel_id=1, replica_groups=mesh['grp'=4,'col'=8] {'col'}, dimensions={1}, use_global_device_ids=true | all-gather | bytes 147456 | tf_op jit(solution)/shard_map/all_gather | solution.py:70
  611.3 9.5 %fusion.34 = f32[16,32,256]{2,0,1:T(8,128)S(1)} fusion(f32[1,1,32,256,256]{4,3,2,1,0:T(8,128)} %param.17, f32[16,32,256]{2,1,0:T(8,128)S(1)} %convolution_bitcast_fusion.4), kind=kOutput, calls=%fused_computation.22 | convolution fusion | flops 402653184 | bytes 9437184 | tf_op jit(solution)/shard_map/sij,qsj->qsi/dot_general | solution.py:74
  621.5 6.6 fusion.37
  630.2 0.7 copy.91
  631.6 20.4 %reduce-scatter.29.cloned.1.call-done = f32[16,256]{1,0:T(8,128)} async-done(((f32[16,1024]{1,0:T(8,128)}), f32[16,256]{1,0:T(8,128)}) %reduce-scatter.29.cloned.1.call-update) | async-done | bytes 16400 | tf_op jit(solution)/shard_map/reduce_scatter | solution.py:53
  652.0 33.3 %reduce-scatter.27.cloned.1.call-done = f32[16,256]{1,0:T(8,128)} async-done(((f32[16,2048]{1,0:T(8,128)}), f32[16,256]{1,0:T(8,128)}) %reduce-scatter.27.cloned.1.call-update) | async-done | bytes 16400 | tf_op jit(solution)/shard_map/reduce_scatter | solution.py:52
  685.3 0.7 add_subtract_fusion
  686.2 37.9 %psum.78 = f32[4,16,16]{1,2,0:T(8,128)S(1)} all-reduce(f32[4,16,16]{1,2,0:T(8,128)S(1)} %convolution_bitcast_fusion.8), channel_id=1, replica_groups=mesh['grp'=4,'col'=8] {'grp','col'}, use_global_device_ids=true, to_apply=%region_22.25 | all-reduce | flops 1024 | bytes 8192 | tf_op jit(solution)/shard_map/psum | solution.py:80
  724.5 41.4 %psum.79 = f32[16,16]{0,1:T(8,128)S(1)} all-reduce(f32[16,16]{0,1:T(8,128)S(1)} %fusion.185), channel_id=1, replica_groups=mesh['grp'=4,'col'=8] {'grp','col'}, use_global_device_ids=true, to_apply=%region_23.26 | all-reduce | flops 256 | bytes 2048 | tf_op jit(solution)/shard_map/psum | solution.py:83
  766.0 1.5 cholesky.133
  768.7 1.2 custom-call.13
  770.0 0.8 copy.65
  (119 shorter events, 26.2 us)
Async XLA Ops:
  7.2 9.0 %copy-start = (f32[16,256]{1,0:T(8,128)S(1)}, f32[16,256]{1,0:T(8,128)}, u32[]{:S(2)}) copy-start(f32[16,256]{1,0:T(8,128)} %param.16) | copy-start | bytes 49156
  7.2 7.3 copy-start.3
  7.2 82.3 %reduce-scatter.33.cloned.1.call-start = ((), (), s32[]{:S(2)}) async-start(), calls=%async_computation.19 | async-start | bytes 655360
  14.4 76.1 %reduce-scatter.31.cloned.1.call-start = ((), (), s32[]{:S(2)}) async-start(), calls=%async_computation.18 | async-start | bytes 1179648
  16.1 87.0 %reduce-scatter.17.cloned.1.call-start = ((), (), s32[]{:S(2)}) async-start(), calls=%async_computation.11 | async-start | bytes 81920 | tf_op jit(solution)/shard_map/reduce_scatter | solution.py:53
  70.0 66.4 %reduce-scatter.15.cloned.1.call-start = ((), (), s32[]{:S(2)}) async-start(), calls=%async_computation.10 | async-start | bytes 147456 | tf_op jit(solution)/shard_map/reduce_scatter | solution.py:52
  88.7 197.8 %reduce-scatter.21.cloned.1.call-start = ((), (), s32[]{:S(2)}) async-start(), calls=%async_computation.13 | async-start | bytes 81920 | tf_op jit(solution)/shard_map/reduce_scatter | solution.py:53
  264.1 55.8 %reduce-scatter.19.cloned.1.call-start = ((), (), s32[]{:S(2)}) async-start(), calls=%async_computation.12 | async-start | bytes 147456 | tf_op jit(solution)/shard_map/reduce_scatter | solution.py:52
  265.5 203.6 %reduce-scatter.25.cloned.1.call-start = ((), (), s32[]{:S(2)}) async-start(), calls=%async_computation.15 | async-start | bytes 81920 | tf_op jit(solution)/shard_map/reduce_scatter | solution.py:53
  446.6 55.9 %reduce-scatter.23.cloned.1.call-start = ((), (), s32[]{:S(2)}) async-start(), calls=%async_computation.14 | async-start | bytes 147456 | tf_op jit(solution)/shard_map/reduce_scatter | solution.py:52
  448.1 203.9 %reduce-scatter.29.cloned.1.call-start = ((), (), s32[]{:S(2)}) async-start(), calls=%async_computation.17 | async-start | bytes 81920 | tf_op jit(solution)/shard_map/reduce_scatter | solution.py:53
  629.5 55.8 %reduce-scatter.27.cloned.1.call-start = ((), (), s32[]{:S(2)}) async-start(), calls=%async_computation.16 | async-start | bytes 147456 | tf_op jit(solution)/shard_map/reduce_scatter | solution.py:52
  771.4 0.6 copy-start.2
  772.0 0.6 copy-start.1
Sparse Core Ops, SparseCore 0:
  14.5 27.8 reduce-scatter.32
  44.6 32.7 reduce-scatter.30
  80.8 22.2 reduce-scatter.16
  105.7 30.5 reduce-scatter.14
  264.2 22.3 reduce-scatter.20
  289.3 30.5 reduce-scatter.18
  446.7 22.3 reduce-scatter.24
  471.9 30.5 reduce-scatter.22
  629.6 22.3 reduce-scatter.28
  654.7 30.5 reduce-scatter.26
